TPU v7x, 32 devices: a whole 2x2x4 slice. The times are simulated.
32 devices in a mesh: parts: 2 (over y), tensor: 4 (over z), dp: 4 (over x, core).
Axes of the slice: x: 2, y: 2, z: 4, core: 2. Of those that a mesh axis runs over, the one named last changes fastest.
Arguments:
- inputs: bfloat16 [4096, 8192], P(('parts', 'dp'), 'tensor'), parts along dimension 0, may hold values from -6 to 6
- cotangent: bfloat16 [4096, 8192], P(('parts', 'dp'), 'tensor'), parts along dimension 0, may hold values from -6 to 6
- weight: bfloat16 [8192, 8192], P(None, 'tensor'), may hold values from -0.0625 to 0.0625
- down_weight_maps: bfloat16 [8192, 2048], P('tensor', 'parts'), parts along dimension 1, may hold values from -0.0625 to 0.0625
- up_weight_maps: bfloat16 [2048, 8192], P('parts', 'tensor'), parts along dimension 0, may hold values from -0.75 to 0.75
- counts: int32 [8, 16], P('parts'), parts along dimension 0, may hold values from 0 to 256, as said below
- ranks: int32 [32], P('parts'), parts along dimension 0, may hold values from 8 to 64, as said below
- owners: int32 [32], P('parts'), parts along dimension 0, may hold values from 0 to 3
Outputs:
- projected: bfloat16 [4096, 8192], P(('parts', 'dp'), 'tensor'), parts along dimension 0
- input_grad: bfloat16 [4096, 8192], P(('parts', 'dp'), 'tensor'), parts along dimension 0
- grad_a: float32 [8, 8192, 1024], P(('parts', 'dp'), 'tensor'), parts along dimension 0
- grad_b: float32 [8, 1024, 8192], P(('parts', 'dp'), None, 'tensor'), parts along dimension 0
There are 2 independent parts, one for each index of `parts`. A program takes and returns all parts, laid end to end along the dimension named above; an argument that names none is the same for every part. Nothing has to cross between parts.
Inputs may be any that keep to these rules, and one draw needn't show every extreme that they name: `counts`: each row sums to at most 512, one row to exactly 512, and all rows together to exactly 1024; some entry is exactly 256. `ranks`: each rank is 64 divided by 1, 2, 4 or 8; some trial has 64 and some 64 // 8.
All inputs are finite; a program needn't handle non-finite values.
Results may differ from a plain program's by a relative error of at most 0.0034.
Values may be sent and summed in bfloat16 or wider, within the bound.
A program may use at most 256 MiB of HBM per device.

v0:
```python
import jax
import jax.numpy as jnp
from jax import lax
from jax.sharding import PartitionSpec as P

LARGEST_RANK = 64
TRIALS = 16
LANES = 128
adapter_alpha = 16.0
TRAILING = (((1,), (1,)), ((), ()))
FIRST = (((0,), (0,)), ((), ()))


def fold_columns(values, match):
    width = values.shape[1]
    kept = jnp.where(match, values, 0.0)
    return sum((kept[:, i : i + LANES] for i in range(0, width, LANES)))


def spread_columns(folded, match):
    repeats = match.shape[1] // LANES
    return jnp.where(
        match, jnp.concatenate([folded] * repeats, axis=1), jnp.zeros((), folded.dtype)
    )


def local(inputs, cotangent, weight, down_weight_maps, up_weight_maps, counts, ranks, owners):
    slot_count, feature_local = inputs.shape
    group_count = counts.shape[0]
    width = down_weight_maps.shape[1]
    column = jnp.arange(width, dtype=jnp.int32)
    col_trial = column // LARGEST_RANK
    column_slot = column % LARGEST_RANK
    trial_ids = jnp.arange(TRIALS, dtype=jnp.int32)
    matches = col_trial[:, None] == trial_ids[None, :]
    rank_per_column = jnp.sum(jnp.where(matches, ranks[None, :], 0), axis=1)
    owner_col = jnp.sum(jnp.where(matches, owners[None, :], 0), axis=1)
    scale_per_column = jnp.where(
        column_slot < rank_per_column, adapter_alpha / rank_per_column.astype(jnp.float32), 0.0
    )
    trial_rows = jnp.sum(counts, axis=0)
    per_trial = 1.0 / jnp.maximum(trial_rows, 1).astype(jnp.float32)
    inverse_col = jnp.sum(jnp.where(matches, per_trial[None, :], 0.0), axis=1)
    cumulative = jnp.cumsum(counts, axis=1)
    group_ids = jnp.arange(group_count, dtype=jnp.int32)
    my_group = lax.axis_index("dp")
    positions = jnp.arange(slot_count, dtype=jnp.int32)
    trial_all = jnp.sum(
        (positions[None, :, None] >= cumulative[:, None, :]).astype(jnp.int32), axis=2
    )
    row_trial = jnp.sum(jnp.where((group_ids == my_group)[:, None], trial_all, 0), axis=0)
    is_live = row_trial < TRIALS
    match = row_trial[:, None] == col_trial[None, :]
    match_all = trial_all.reshape(-1)[:, None] == col_trial[None, :]
    coef = jnp.where(match, scale_per_column[None, :], 0.0)
    coef_folded = fold_columns(coef, match)
    down_part = jnp.dot(inputs, down_weight_maps, preferred_element_type=jnp.float32)
    back_part = lax.dot_general(
        cotangent, up_weight_maps, TRAILING, preferred_element_type=jnp.float32
    )
    folded = jnp.concatenate(
        [fold_columns(down_part, match), fold_columns(back_part, match)], axis=1
    )
    folded = lax.psum(folded, "tensor")
    scaled_down_f = (coef_folded * folded[:, :LANES]).astype(jnp.bfloat16)
    scaled_back_f = (coef_folded * folded[:, LANES:]).astype(jnp.bfloat16)
    all_inputs = lax.all_gather(inputs, "tensor", axis=1, tiled=True)
    mine = lax.axis_index("tensor")
    block = jnp.arange(weight.shape[0], dtype=jnp.int32) // feature_local
    frozen_back = lax.dot_general(cotangent, weight, TRAILING, preferred_element_type=jnp.float32)
    others = jnp.where((block == mine)[None, :], 0.0, frozen_back).astype(jnp.bfloat16)
    others_share = lax.psum_scatter(others, "tensor", scatter_dimension=1, tiled=True)
    own_weight = lax.dynamic_slice_in_dim(weight, mine * feature_local, feature_local, 0)
    own_share = lax.dot_general(cotangent, own_weight, TRAILING, preferred_element_type=jnp.float32)
    frozen_share = own_share + others_share.astype(jnp.float32)
    group_inputs = lax.all_gather(inputs, "dp", axis=0, tiled=True)
    group_cotangent = lax.all_gather(cotangent, "dp", axis=0, tiled=True)
    both = lax.all_gather(
        jnp.concatenate([scaled_down_f, scaled_back_f], axis=1), "dp", axis=0, tiled=True
    )
    frozen_output = jnp.dot(all_inputs, weight, preferred_element_type=jnp.float32)
    scaled_down = spread_columns(scaled_down_f, match)
    scaled_back = spread_columns(scaled_back_f, match)
    merged = frozen_output + jnp.dot(
        scaled_down, up_weight_maps, preferred_element_type=jnp.float32
    )
    projected = jnp.where(is_live[:, None], merged, 0.0).astype(jnp.bfloat16)
    adapter_in = lax.dot_general(
        scaled_back, down_weight_maps, TRAILING, preferred_element_type=jnp.float32
    )
    input_grad = jnp.where(is_live[:, None], frozen_share + adapter_in, 0.0).astype(jnp.bfloat16)
    owned = jnp.where(owner_col == my_group, inverse_col, 0.0)
    down_all = spread_columns(both[:, :LANES], match_all)
    back_all = spread_columns(both[:, LANES:], match_all)
    grad_a = lax.dot_general(group_inputs, back_all, FIRST, preferred_element_type=jnp.float32)
    grad_b = lax.dot_general(down_all, group_cotangent, FIRST, preferred_element_type=jnp.float32)
    grad_a = (grad_a * owned[None, :])[None]
    grad_b = (grad_b * owned[:, None])[None]
    return (projected, input_grad, grad_a, grad_b)


def solution(mesh):
    return jax.shard_map(
        local,
        mesh=mesh,
        in_specs=(
            P(("parts", "dp"), "tensor"),
            P(("parts", "dp"), "tensor"),
            P(None, "tensor"),
            P("tensor", "parts"),
            P("parts", "tensor"),
            P("parts", None),
            P("parts"),
            P("parts"),
        ),
        out_specs=(
            P(("parts", "dp"), "tensor"),
            P(("parts", "dp"), "tensor"),
            P(("parts", "dp"), "tensor", None),
            P(("parts", "dp"), None, "tensor"),
        ),
        check_vma=False,
    )
```

profile of v0, /device:TPU:0, one launch (start us, length us, event | category | flops | bytes accessed | tf_op | source)
XLA Modules:
  0.0 511.5 jit_solution(14548352022868119628)
XLA Ops:
  8.3 5.3 %compare_select_fusion.4 = f32[512,1024]{1,0:T(8,128)S(1)} fusion(bf16[512,2048]{1,0:T(8,128)(2,1)} %param.9, bf16[1024,2048]{1,0:T(8,128)(2,1)} %param.12, s32[1024]{0:T(1024)S(1)} %add_select_fusion.1, s32[512]{0:T(512)S(1)} %select_reduce_fusion.3), kind=kOutput, calls=%fused_computation.9 | convolution fusion | flops 2148532224 | bytes 8394752 | tf_op jit(solution)/shard_map/dot_general | solution.py:58
  13.8 2.3 compare_select_fusion.5
  17.6 40.7 %all-reduce.2.cloned.1.call-done = f32[512,256]{1,0:T(8,128)} async-done(((f32[512,256]{1,0:T(8,128)}), f32[512,256]{1,0:T(8,128)}) %all-reduce.2.cloned.1.call-update) | async-done | bytes 524304 | tf_op jit(solution)/shard_map/psum | solution.py:64
  58.2 1.1 constant_dynamic-update-slice_fusion.15
  59.3 1.8 constant_dynamic-update-slice_fusion.7
  64.0 24.4 %select_convert_fusion = bf16[512,8192]{1,0:T(8,128)(2,1)} fusion(bf16[512,2048]{1,0:T(8,128)(2,1)S(1)} %copy-done.2, bf16[8192,2048]{1,0:T(8,128)(2,1)} %param.10, pred[8192]{0:T(1024)(128)(4,1)S(1)} %fusion.23), kind=kOutput, calls=%fused_computation | convolution fusion | flops 17188257792 | bytes 44048384 | tf_op jit(solution)/shard_map/dot_general | solution.py:70
  89.6 7.7 %fusion.14 = f32[512,2048]{1,0:T(8,128)} fusion(bf16[2048,1024]{1,0:T(8,128)(2,1)} %param.11, bf16[512,1024]{1,0:T(8,128)(2,1)S(1)} %constant_dynamic-update-slice_fusion.8, s32[1024]{0:T(1024)S(1)} %add_select_fusion.1, s32[512]{0:T(512)S(1)} %select_reduce_fusion.3), kind=kOutput, calls=%fused_computation.25 | convolution fusion | flops 2148532224 | bytes 9443328 | tf_op jit(solution)/shard_map/dot_general | solution.py:88
  97.6 4.4 fusion.13
  102.0 2.0 slice_dynamic-update-slice_fusion.6
  104.0 2.0 slice_dynamic-update-slice_fusion.5
  106.0 1.9 slice_dynamic-update-slice_fusion.4
  107.9 1.9 slice_dynamic-update-slice_fusion.3
  110.6 0.9 slice_dynamic-update-slice_fusion.1
  111.5 0.9 slice_dynamic-update-slice_fusion
  112.4 1.0 slice_dynamic-update-slice_fusion.7
  119.2 19.4 %all-gather.9.cloned.1.call-done = bf16[2048,2048]{1,0:T(8,128)(2,1)} async-done(((bf16[512,2048]{1,0:T(8,128)(2,1)}), bf16[2048,2048]{1,0:T(8,128)(2,1)}) %all-gather.9.cloned.1.call-update) | async-done | bytes 8388624 | tf_op jit(solution)/shard_map/all_gather | solution.py:76
  138.6 14.9 %multiply_bitcast_fusion.1 = f32[1,2048,1024]{1,2,0:T(8,128)} fusion(bf16[2048,2048]{1,0:T(8,128)(2,1)} %all-gather.9.cloned.1.call-done, bf16[2048,1024]{1,0:T(8,128)(2,1)} %slice_dynamic-update-slice_fusion.15, f32[1024]{0:T(1024)S(1)} %compare_select_fusion.12, s32[1024]{0:T(1024)S(1)} %add_select_fusion.1, s32[2048]{0:T(1024)S(1)} %bitcast.30), kind=kOutput, calls=%fused_computation.4 | convolution fusion | flops 8596226048 | bytes 20987904 | tf_op jit(solution)/shard_map/dot_general | solution.py:95
  153.5 9.2 %copy.15 = f32[1,2048,1024]{2,1,0:T(8,128)} copy(f32[1,2048,1024]{1,2,0:T(8,128)} %multiply_bitcast_fusion.1) | data formatting | bytes 16777216
  162.7 35.6 %all-gather.11.cloned.1.call-done = bf16[2048,2048]{1,0:T(8,128)(2,1)} async-done(((bf16[512,2048]{1,0:T(8,128)(2,1)}), bf16[2048,2048]{1,0:T(8,128)(2,1)}) %all-gather.11.cloned.1.call-update) | async-done | bytes 8388624 | tf_op jit(solution)/shard_map/all_gather | solution.py:77
  198.3 14.9 %multiply_bitcast_fusion = f32[1,1024,2048]{2,1,0:T(8,128)} fusion(bf16[2048,2048]{1,0:T(8,128)(2,1)} %all-gather.11.cloned.1.call-done, bf16[2048,1024]{1,0:T(8,128)(2,1)} %get-tuple-element.19, f32[1024]{0:T(1024)S(1)} %compare_select_fusion.12, s32[1024]{0:T(1024)S(1)} %add_select_fusion.1, s32[2048]{0:T(1024)S(1)} %bitcast.31), kind=kOutput, calls=%fused_computation.3 | convolution fusion | flops 8596226048 | bytes 20987904 | tf_op jit(solution)/shard_map/dot_general | solution.py:96
  213.2 136.2 %all-gather.5.cloned.1.call-done = bf16[512,8192]{1,0:T(8,128)(2,1)} async-done(((bf16[512,2048]{1,0:T(8,128)(2,1)}), bf16[512,8192]{1,0:T(8,128)(2,1)}) %all-gather.5.cloned.1.call-update) | async-done | bytes 8388624 | tf_op jit(solution)/shard_map/all_gather | solution.py:67
  349.4 24.9 %select_convert_fusion.1 = bf16[512,2048]{1,0:T(8,128)(2,1)} fusion(f32[512,2048]{1,0:T(8,128)} %fusion.13, bf16[512,8192]{1,0:T(8,128)(2,1)} %all-gather.5.cloned.1.call-done, bf16[8192,2048]{1,0:T(8,128)(2,1)} %param.10, pred[512]{0:T(512)(128)(4,1)S(1)} %broadcast_compare_fusion), kind=kOutput, calls=%fused_computation.19 | convolution fusion | flops 17183014912 | bytes 48235008 | tf_op jit(solution)/shard_map/dot_general | solution.py:81
  374.3 120.0 %reduce-scatter.2.cloned.1.call-done = bf16[512,2048]{1,0:T(8,128)(2,1)} async-done(((bf16[512,8192]{1,0:T(8,128)(2,1)}), bf16[512,2048]{1,0:T(8,128)(2,1)}) %reduce-scatter.2.cloned.1.call-update) | async-done | bytes 2097168 | tf_op jit(solution)/shard_map/reduce_scatter | solution.py:72
  494.3 10.3 %fusion.4 = bf16[512,2048]{1,0:T(8,128)(2,1)} fusion(f32[512,2048]{1,0:T(8,128)} %fusion.14, bf16[512,2048]{1,0:T(8,128)(2,1)} %reduce-scatter.2.cloned.1.call-done, bf16[512,2048]{1,0:T(8,128)(2,1)S(1)} %copy-done.2, bf16[8192,2048]{1,0:T(8,128)(2,1)} %param.10, s32[]{:T(128)S(6)} %select_n.128, pred[512]{0:T(512)(128)(4,1)S(1)} %broadcast_compare_fusion), kind=kOutput, calls=%fused_computation.16 | convolution fusion | flops 4300210176 | bytes 18874884 | tf_op jit(solution)/shard_map/dot_general | solution.py:74
  (72 shorter events, 13.4 us)
Async XLA Ops:
  7.2 51.1 %all-reduce.2.cloned.1.call-start = ((), (), s32[]{:S(2)}) async-start(), calls=%async_computation.2 | async-start | bytes 1048576 | tf_op jit(solution)/shard_map/psum | solution.py:64
  8.3 5.5 %copy-start.1 = (bf16[512,2048]{1,0:T(8,128)(2,1)S(1)}, bf16[512,2048]{1,0:T(8,128)(2,1)}, u32[]{:S(2)}) copy-start(bf16[512,2048]{1,0:T(8,128)(2,1)} %param.8) | copy-start | bytes 6291460
  8.3 5.5 %copy-start.7 = (bf16[2048,1024]{1,0:T(8,128)(2,1)S(1)}, bf16[2048,1024]{1,0:T(8,128)(2,1)}, u32[]{:S(2)}) copy-start(bf16[2048,1024]{1,0:T(8,128)(2,1)} %param.11) | copy-start | bytes 12582916
  13.8 3.4 copy-start.5
  13.8 3.4 copy-start.6
  17.1 84.9 %all-gather.7.cloned.1.call-start = ((), (), s32[]{:S(2)}) async-start(), calls=%async_computation.4 | async-start | bytes 1310720 | tf_op jit(solution)/shard_map/all_gather | solution.py:78
  59.3 4.7 copy-start.2
  61.8 76.8 %all-gather.9.cloned.1.call-start = ((), (), s32[]{:S(2)}) async-start(), calls=%async_computation.5 | async-start | bytes 10485760 | tf_op jit(solution)/shard_map/all_gather | solution.py:76
  62.6 135.8 %all-gather.11.cloned.1.call-start = ((), (), s32[]{:S(2)}) async-start(), calls=%async_computation.6 | async-start | bytes 10485760 | tf_op jit(solution)/shard_map/all_gather | solution.py:77
  63.2 286.3 %all-gather.5.cloned.1.call-start = ((), (), s32[]{:S(2)}) async-start(), calls=%async_computation.1 | async-start | bytes 10485760 | tf_op jit(solution)/shard_map/all_gather | solution.py:67
  63.8 430.6 %reduce-scatter.2.cloned.1.call-start = ((), (), s32[]{:S(2)}) async-start(), calls=%async_computation.3 | async-start | bytes 10485760 | tf_op jit(solution)/shard_map/reduce_scatter | solution.py:72
  88.4 0.7 copy-start.4
  89.5 7.7 %copy-start.3 = (bf16[512,1024]{1,0:T(8,128)(2,1)S(1)}, bf16[512,1024]{1,0:T(8,128)(2,1)}, u32[]{:S(2)}) copy-start(bf16[512,1024]{1,0:T(8,128)(2,1)} %get-tuple-element.17) | copy-start | bytes 3145732
  89.5 8.0 %copy-start.8 = (bf16[1024,2048]{1,0:T(8,128)(2,1)S(1)}, bf16[1024,2048]{1,0:T(8,128)(2,1)}, u32[]{:S(2)}) copy-start(bf16[1024,2048]{1,0:T(8,128)(2,1)} %param.12) | copy-start | bytes 12582916
  102.0 7.8 %copy-start = (bf16[2048,256]{1,0:T(8,128)(2,1)S(1)}, bf16[2048,256]{1,0:T(8,128)(2,1)}, u32[]{:S(2)}) copy-start(bf16[2048,256]{1,0:T(8,128)(2,1)} %all-gather.7.cloned.1.call-done) | copy-start | bytes 3145732
Sparse Core Ops, SparseCore 0:
  17.2 40.9 all-reduce.1
  62.0 16.6 all-gather.6
  80.3 58.2 all-gather.8
  140.0 58.2 all-gather.10
  199.8 149.6 all-gather.4
  351.6 142.6 reduce-scatter.1
where the time goes:
time: 512 us; the launch traced here: 511 us
  waiting for transfers between devices  354 us (69%)
  matrix products  109 us (21%)
  local copies, waits for them, and re-layouts  27.7 us (5%)
  between operations  14.4 us (3%)
  other arithmetic  6.18 us (1%)
    all_gather x1, waiting for transfers between devices, local(): all_inputs = lax.all_gather(inputs, 'tensor', axis=1, tiled=True)  136 us
    reduce_scatter x1, waiting for transfers between devices, local(): lax.psum_scatter(others, 'tensor', scatter_dimension=1, tiled=True)  120 us
    psum x1, waiting for transfers between devices, local(): folded = lax.psum(folded, 'tensor')  40.7 us
    all_gather x1, waiting for transfers between devices, local(): group_cotangent = lax.all_gather(cotangent, 'dp', axis=0, tiled=True)  35.6 us
    unnamed x45, local copies, waits for them, and re-layouts  25.8 us
    dot_general x1, matrix products, local(): jnp.dot(all_inputs, weight, preferred_element_type=jnp.float32)  24.9 us
    dot_general x1, matrix products, local(): lax.dot_general(cotangent, weight, TRAILING, preferred_element_type=jnp.f...  24.4 us
    all_gather x1, waiting for transfers between devices, local(): group_inputs = lax.all_gather(inputs, 'dp', axis=0, tiled=True)  19.4 us
  transfers between devices with their start and end apart: 6, of which 5 were waited for; matrix products, arithmetic and copies ran while one was open for 23% of the time, Pallas kernels for 0%

commit v1 on v0

--- a/solution.py
+++ b/solution.py
@@ -64,7 +64,24 @@
     folded = lax.psum(folded, "tensor")
     scaled_down_f = (coef_folded * folded[:, :LANES]).astype(jnp.bfloat16)
     scaled_back_f = (coef_folded * folded[:, LANES:]).astype(jnp.bfloat16)
-    all_inputs = lax.all_gather(inputs, "tensor", axis=1, tiled=True)
+    ways, here, step = (lax.axis_size("tensor"), lax.axis_index("tensor"), inputs.shape[1])
+    dims = [n * ways if d == 1 else n for d, n in enumerate(inputs.shape)]
+    all_inputs = lax.dynamic_update_slice_in_dim(
+        jnp.zeros(dims, inputs.dtype), inputs, here * step, axis=1
+    )
+    going_up = going_down = inputs
+    for far in range(1, ways // 2 + 1):
+        going_up = lax.ppermute(going_up, "tensor", [(d, (d + 1) % ways) for d in range(ways)])
+        all_inputs = lax.dynamic_update_slice_in_dim(
+            all_inputs, going_up, (here - far) % ways * step, axis=1
+        )
+        if 2 * far < ways:
+            going_down = lax.ppermute(
+                going_down, "tensor", [(d, (d - 1) % ways) for d in range(ways)]
+            )
+            all_inputs = lax.dynamic_update_slice_in_dim(
+                all_inputs, going_down, (here + far) % ways * step, axis=1
+            )
     mine = lax.axis_index("tensor")
     block = jnp.arange(weight.shape[0], dtype=jnp.int32) // feature_local
     frozen_back = lax.dot_general(cotangent, weight, TRAILING, preferred_element_type=jnp.float32)

time: 512 us -> 363 us (0.71)
  waiting for transfers between devices: 354 us -> 187 us
  local copies, waits for them, and re-layouts: 27.7 us -> 39.3 us
    all_gather x1 -> x0, waiting for transfers between devices: 136 us -> none  [local(): all_inputs = lax.all_gather(inputs, 'tensor', axis=1, tiled=True)]
    ppermute x0 -> x3, waiting for transfers between devices: none -> 70.3 us  [the longest x2 38.7 us: local(): lax.ppermute(going_up, 'tensor', [(d, (d + 1) % ways) for d in range(ways)])]
    reduce_scatter x1, waiting for transfers between devices: 120 us -> 75.9 us  [local(): lax.psum_scatter(others, 'tensor', scatter_dimension=1, tiled=True)]
    all_gather x1, waiting for transfers between devices: 35.6 us -> 0.01 us  [local(): group_cotangent = lax.all_gather(cotangent, 'dp', axis=0, tiled=True)]
    all_gather x1, waiting for transfers between devices: 19.4 us -> 0.01 us  [local(): group_inputs = lax.all_gather(inputs, 'dp', axis=0, tiled=True)]
    dynamic_update_slice x0 -> x4, local copies, waits for them, and re-layouts: none -> 11.1 us  [the longest x2 6.32 us: local(): lax.dynamic_update_slice_in_dim(all_inputs, going_up, (here - far) % ways...]
    unnamed x45 -> x51, local copies, waits for them, and re-layouts: 25.8 us -> 22.7 us
  transfers between devices with their start and end apart: 6 -> 8, of which waited for: 5 -> 4; matrix products, arithmetic and copies ran while one was open for 23% -> 36% of each run, Pallas kernels for 0% -> 0%
where the time goes in v1:
time: 363 us; the launch traced here: 362 us
  waiting for transfers between devices  187 us (52%)
  matrix products  110 us (30%)
  local copies, waits for them, and re-layouts  39.3 us (11%)
  between operations  14.2 us (4%)
  other arithmetic  8.02 us (2%)
  starting transfers between devices  4.08 us (1%)
    reduce_scatter x1, waiting for transfers between devices, local(): lax.psum_scatter(others, 'tensor', scatter_dimension=1, tiled=True)  75.9 us
    psum x1, waiting for transfers between devices, local(): folded = lax.psum(folded, 'tensor')  39.4 us
    ppermute x2, waiting for transfers between devices, local(): lax.ppermute(going_up, 'tensor', [(d, (d + 1) % ways) for d in range(ways)])  38.7 us
    ppermute x1, waiting for transfers between devices, local(): lax.ppermute(going_down, 'tensor', [(d, (d - 1) % ways) for d in range(wa...  31.5 us
    dot_general x1, matrix products, local(): jnp.dot(all_inputs, weight, preferred_element_type=jnp.float32)  25.4 us
    dot_general x1, matrix products, local(): lax.dot_general(cotangent, weight, TRAILING, preferred_element_type=jnp.f...  25.2 us
    unnamed x51, local copies, waits for them, and re-layouts  22.7 us
    dot_general x1, matrix products, local(): lax.dot_general(down_all, group_cotangent, FIRST, preferred_element_type=...  15 us
  transfers between devices with their start and end apart: 8, of which 4 were waited for; matrix products, arithmetic and copies ran while one was open for 36% of the time, Pallas kernels for 0%

profile of v1, /device:TPU:0, one launch (start us, length us, event | category | flops | bytes accessed | tf_op | source)
XLA Modules:
  0.0 362.4 jit_solution(2097231501993026895)
XLA Ops:
  8.3 5.3 %compare_select_fusion.4 = f32[512,1024]{1,0:T(8,128)S(1)} fusion(bf16[512,2048]{1,0:T(8,128)(2,1)} %param.9, bf16[1024,2048]{1,0:T(8,128)(2,1)} %param.12, s32[1024]{0:T(1024)S(1)} %add_select_fusion.1, s32[512]{0:T(512)S(1)} %select_reduce_fusion.3), kind=kOutput, calls=%fused_computation.9 | convolution fusion | flops 2148532224 | bytes 8394752 | tf_op jit(solution)/shard_map/dot_general | solution.py:58
  13.8 2.3 compare_select_fusion.5
  17.3 1.6 compare_select_fusion.6
  18.9 39.4 %all-reduce.2.cloned.1.call-done = f32[512,256]{1,0:T(8,128)} async-done(((f32[512,256]{1,0:T(8,128)}), f32[512,256]{1,0:T(8,128)}) %all-reduce.2.cloned.1.call-update) | async-done | bytes 524304 | tf_op jit(solution)/shard_map/psum | solution.py:64
  58.2 1.7 constant_dynamic-update-slice_fusion.15
  60.0 1.6 constant_dynamic-update-slice_fusion.7
  65.0 2.6 collective-permute-start.1
  67.6 25.2 %select_convert_fusion = bf16[512,8192]{1,0:T(8,128)(2,1)} fusion(bf16[512,2048]{1,0:T(8,128)(2,1)} %param.9, bf16[8192,2048]{1,0:T(8,128)(2,1)} %param.10, pred[8192]{0:T(1024)(128)(4,1)S(1)} %fusion.23), kind=kOutput, calls=%fused_computation | convolution fusion | flops 17188257792 | bytes 44048384 | tf_op jit(solution)/shard_map/dot_general | solution.py:87
  93.7 4.4 %broadcast_in_dim.130 = bf16[512,8192]{1,0:T(8,128)(2,1)} broadcast(bf16[]{:T(256)} %constant.82.clone.1), dimensions={} | broadcast | bytes 8388610 | tf_op jit(solution)/shard_map/broadcast_in_dim | solution.py:70
  98.1 1.6 constant_dynamic-update-slice_fusion.19
  104.7 7.1 %fusion.13 = f32[512,2048]{1,0:T(8,128)} fusion(bf16[1024,2048]{1,0:T(8,128)(2,1)} %param.12, bf16[512,1024]{1,0:T(8,128)(2,1)} %constant_dynamic-update-slice_fusion, s32[1024]{0:T(1024)S(1)} %add_select_fusion.1, s32[512]{0:T(512)S(1)} %select_reduce_fusion.3), kind=kOutput, calls=%fused_computation.24 | convolution fusion | flops 2148532224 | bytes 9443328 | tf_op jit(solution)/shard_map/dot_general | solution.py:101
  111.7 4.4 %fusion.14 = f32[512,2048]{1,0:T(8,128)} fusion(bf16[2048,1024]{1,0:T(8,128)(2,1)S(1)} %copy-done.10, bf16[512,1024]{1,0:T(8,128)(2,1)S(1)} %constant_dynamic-update-slice_fusion.8, s32[1024]{0:T(1024)S(1)} %add_select_fusion.1, s32[512]{0:T(512)S(1)} %select_reduce_fusion.3), kind=kOutput, calls=%fused_computation.25 | convolution fusion | flops 2148532224 | bytes 9443328 | tf_op jit(solution)/shard_map/dot_general | solution.py:105
  121.7 3.2 constant_dynamic-update-slice_fusion.18
  125.8 31.5 %collective-permute-done.1 = bf16[512,2048]{1,0:T(8,128)(2,1)} collective-permute-done((bf16[512,2048]{1,0:T(8,128)(2,1)S(1)}, bf16[512,2048]{1,0:T(8,128)(2,1)}, u32[]{:S(2)}, u32[]{:S(2)}) %collective-permute-start.1) | collective-permute-done | bytes 2097184 | tf_op jit(solution)/shard_map/ppermute | solution.py:79
  157.3 3.2 constant_dynamic-update-slice_fusion.17
  161.2 2.1 copy-done.5
  163.3 38.7 %collective-permute-done.2 = bf16[512,2048]{1,0:T(8,128)(2,1)} collective-permute-done((bf16[512,2048]{1,0:T(8,128)(2,1)}, bf16[512,2048]{1,0:T(8,128)(2,1)}, u32[]{:S(2)}, u32[]{:S(2)}) %collective-permute-start.2) | collective-permute-done | bytes 2097184 | tf_op jit(solution)/shard_map/ppermute | solution.py:74
  202.0 3.2 constant_dynamic-update-slice_fusion.16
  205.2 25.4 %select_convert_fusion.1 = bf16[512,2048]{1,0:T(8,128)(2,1)} fusion(f32[512,2048]{1,0:T(8,128)S(1)} %copy-done.11, bf16[512,8192]{1,0:T(8,128)(2,1)} %constant_dynamic-update-slice_fusion.16, bf16[8192,2048]{1,0:T(8,128)(2,1)} %param.10, pred[512]{0:T(512)(128)(4,1)S(1)} %broadcast_compare_fusion), kind=kOutput, calls=%fused_computation.19 | convolution fusion | flops 17183014912 | bytes 48235008 | tf_op jit(solution)/shard_map/dot_general | solution.py:98
  230.5 14.9 %multiply_bitcast_fusion.1 = f32[1,2048,1024]{1,2,0:T(8,128)} fusion(bf16[2048,2048]{1,0:T(8,128)(2,1)} %all-gather.6.cloned.1.call-done, bf16[2048,1024]{1,0:T(8,128)(2,1)} %copy-done.5, f32[1024]{0:T(1024)S(1)} %compare_select_fusion.12, s32[1024]{0:T(1024)S(1)} %add_select_fusion.1, s32[2048]{0:T(1024)S(1)} %bitcast.30), kind=kOutput, calls=%fused_computation.4 | convolution fusion | flops 8596226048 | bytes 20987904 | tf_op jit(solution)/shard_map/dot_general | solution.py:112
  245.4 9.2 %copy.15 = f32[1,2048,1024]{2,1,0:T(8,128)} copy(f32[1,2048,1024]{1,2,0:T(8,128)} %multiply_bitcast_fusion.1) | data formatting | bytes 16777216
  254.6 15.0 %multiply_bitcast_fusion = f32[1,1024,2048]{2,1,0:T(8,128)} fusion(bf16[2048,2048]{1,0:T(8,128)(2,1)} %all-gather.8.cloned.1.call-done, bf16[2048,1024]{1,0:T(8,128)(2,1)} %copy-done.4, f32[1024]{0:T(1024)S(1)} %compare_select_fusion.12, s32[1024]{0:T(1024)S(1)} %add_select_fusion.1, s32[2048]{0:T(1024)S(1)} %bitcast.31), kind=kOutput, calls=%fused_computation.3 | convolution fusion | flops 8596226048 | bytes 20987904 | tf_op jit(solution)/shard_map/dot_general | solution.py:113
  269.7 75.9 %reduce-scatter.2.cloned.1.call-done = bf16[512,2048]{1,0:T(8,128)(2,1)} async-done(((bf16[512,8192]{1,0:T(8,128)(2,1)}), bf16[512,2048]{1,0:T(8,128)(2,1)}) %reduce-scatter.2.cloned.1.call-update) | async-done | bytes 2097168 | tf_op jit(solution)/shard_map/reduce_scatter | solution.py:89
  345.6 10.3 %fusion.4 = bf16[512,2048]{1,0:T(8,128)(2,1)} fusion(f32[512,2048]{1,0:T(8,128)} %fusion.14, bf16[512,2048]{1,0:T(8,128)(2,1)} %reduce-scatter.2.cloned.1.call-done, bf16[512,2048]{1,0:T(8,128)(2,1)S(1)} %copy-done.3, bf16[8192,2048]{1,0:T(8,128)(2,1)} %param.10, s32[]{:T(128)S(6)} %select_n.142, pred[512]{0:T(512)(128)(4,1)S(1)} %broadcast_compare_fusion), kind=kOutput, calls=%fused_computation.16 | convolution fusion | flops 4300210176 | bytes 18874884 | tf_op jit(solution)/shard_map/dot_general | solution.py:91
  (86 shorter events, 18.4 us)
Async XLA Ops:
  7.2 51.1 %all-reduce.2.cloned.1.call-start = ((), (), s32[]{:S(2)}) async-start(), calls=%async_computation.1 | async-start | bytes 1048576 | tf_op jit(solution)/shard_map/psum | solution.py:64
  8.3 5.5 %copy-start.1 = (bf16[512,2048]{1,0:T(8,128)(2,1)S(1)}, bf16[512,2048]{1,0:T(8,128)(2,1)}, u32[]{:S(2)}) copy-start(bf16[512,2048]{1,0:T(8,128)(2,1)} %param.8) | copy-start | bytes 6291460
  8.3 5.5 %copy-start.9 = (bf16[2048,1024]{1,0:T(8,128)(2,1)S(1)}, bf16[2048,1024]{1,0:T(8,128)(2,1)}, u32[]{:S(2)}) copy-start(bf16[2048,1024]{1,0:T(8,128)(2,1)} %param.11) | copy-start | bytes 12582916
  13.8 3.4 copy-start.7
  13.8 3.4 copy-start.8
  17.1 99.1 %all-gather.4.cloned.1.call-start = ((), (), s32[]{:S(2)}) async-start(), calls=%async_computation.3 | async-start | bytes 1310720 | tf_op jit(solution)/shard_map/all_gather | solution.py:95
  18.9 44.9 %copy-start.2 = (bf16[512,2048]{1,0:T(8,128)(2,1)S(1)}, bf16[512,2048]{1,0:T(8,128)(2,1)}, u32[]{:S(2)}) copy-start(bf16[512,2048]{1,0:T(8,128)(2,1)} %param.8) | copy-start | bytes 6291460
  62.4 168.2 %all-gather.6.cloned.1.call-start = ((), (), s32[]{:S(2)}) async-start(), calls=%async_computation.4 | async-start | bytes 10485760 | tf_op jit(solution)/shard_map/all_gather | solution.py:93
  63.1 191.6 %all-gather.8.cloned.1.call-start = ((), (), s32[]{:S(2)}) async-start(), calls=%async_computation.5 | async-start | bytes 10485760 | tf_op jit(solution)/shard_map/all_gather | solution.py:94
  63.7 281.9 %reduce-scatter.2.cloned.1.call-start = ((), (), s32[]{:S(2)}) async-start(), calls=%async_computation.2 | async-start | bytes 10485760 | tf_op jit(solution)/shard_map/reduce_scatter | solution.py:89
  63.7 52.4 %collective-permute-start = (bf16[512,2048]{1,0:T(8,128)(2,1)S(1)}, bf16[512,2048]{1,0:T(8,128)(2,1)}, u32[]{:S(2)}, u32[]{:S(2)}) collective-permute-start(bf16[512,2048]{1,0:T(8,128)(2,1)S(1)} %copy-done.2), channel_id=1, source_target_pairs={{0,4},{4,8},{8,12},{12,0},{1,5},{5,9},{9,13},{13,1},{2,6},{6,10},{... | collective-permute-start | bytes 6291464 | tf_op jit(solution)/shard_map/ppermute | solution.py:74
  65.0 92.3 %collective-permute-start.1 = (bf16[512,2048]{1,0:T(8,128)(2,1)S(1)}, bf16[512,2048]{1,0:T(8,128)(2,1)}, u32[]{:S(2)}, u32[]{:S(2)}) collective-permute-start(bf16[512,2048]{1,0:T(8,128)(2,1)S(1)} %copy-done.2), channel_id=1, source_target_pairs={{0,12},{4,0},{8,4},{12,8},{1,13},{5,1},{9,5},{13,9},{2,14},{6,2},{... | collective-permute-start | bytes 6291464 | tf_op jit(solution)/shard_map/ppermute | solution.py:79
  92.9 0.7 copy-start.6
  104.6 7.1 %copy-start.10 = (bf16[2048,1024]{1,0:T(8,128)(2,1)S(1)}, bf16[2048,1024]{1,0:T(8,128)(2,1)}, u32[]{:S(2)}) copy-start(bf16[2048,1024]{1,0:T(8,128)(2,1)} %param.11) | copy-start | bytes 12582916
  116.2 85.8 %collective-permute-start.2 = (bf16[512,2048]{1,0:T(8,128)(2,1)}, bf16[512,2048]{1,0:T(8,128)(2,1)}, u32[]{:S(2)}, u32[]{:S(2)}) collective-permute-start(bf16[512,2048]{1,0:T(8,128)(2,1)} %collective-permute-done), channel_id=1, source_target_pairs={{0,4},{4,8},{8,12},{12,0},{1,5},{5,9},{9,13},{13,1},{2,6},{6,10},{... | collective-permute-start | bytes 6291464 | tf_op jit(solution)/shard_map/ppermute | solution.py:74
  116.2 5.0 %copy-start = (bf16[2048,256]{1,0:T(8,128)(2,1)S(1)}, bf16[2048,256]{1,0:T(8,128)(2,1)}, u32[]{:S(2)}) copy-start(bf16[2048,256]{1,0:T(8,128)(2,1)} %all-gather.4.cloned.1.call-done) | copy-start | bytes 3145732
  125.2 35.5 %copy-start.4 = (bf16[2048,1024]{1,0:T(8,128)(2,1)}, bf16[2048,1024]{1,0:T(8,128)(2,1)S(1)}, u32[]{:S(2)}) copy-start(bf16[2048,1024]{1,0:T(8,128)(2,1)S(1)} %get-tuple-element.19) | copy-start | bytes 12582916
  160.5 44.7 %copy-start.11 = (f32[512,2048]{1,0:T(8,128)S(1)}, f32[512,2048]{1,0:T(8,128)}, u32[]{:S(2)}) copy-start(f32[512,2048]{1,0:T(8,128)} %fusion.13) | copy-start | bytes 12582916
  161.2 2.1 copy-start.5
  254.6 90.9 %copy-start.3 = (bf16[512,2048]{1,0:T(8,128)(2,1)S(1)}, bf16[512,2048]{1,0:T(8,128)(2,1)}, u32[]{:S(2)}) copy-start(bf16[512,2048]{1,0:T(8,128)(2,1)} %param.9) | copy-start | bytes 6291460
Sparse Core Ops, SparseCore 0:
  17.2 40.9 all-reduce.1
  62.5 16.6 all-gather.3
  80.8 58.2 all-gather.5
  140.5 58.2 all-gather.7
  201.0 144.4 reduce-scatter.1
